TPU v7x, 32 devices: a whole 2x2x4 slice. The times are simulated.
32 devices in a mesh: seq: 4 (over x, core), dp: 8 (over z, y).
Axes of the slice: x: 2, y: 2, z: 4, core: 2. Of those that a mesh axis runs over, the one named last changes fastest.
Arguments:
- attn_mix: bfloat16 [8, 512, 640], P('dp', 'seq'), may hold values from -6 to 6
- resid: bfloat16 [8, 512, 1280], P('dp', 'seq'), may hold values from -6 to 6
- out_weight: bfloat16 [640, 1280], P('dp'), may hold values from -0.25 to 0.25
- merger_norm_gain: float32 [1280], replicated, may hold values from 0.4 to 1.6
- merger_norm_bias: float32 [1280], replicated, may hold values from -1.5 to 1.5
- target: int32 [8, 128], P('dp'), may hold values from 0 to 511, as said below
- token_grad: bfloat16 [8, 512, 5120], P('dp', 'seq'), may hold values from -6 to 6
Outputs:
- token_rows: bfloat16 [8, 512, 5120], P('dp', 'seq')
- resid_grad: bfloat16 [8, 512, 1280], P('dp', 'seq')
- attn_grad: bfloat16 [8, 512, 640], P('dp', 'seq')
Inputs may be any that keep to these rules, and one draw needn't show every extreme that they name: `target`: within one packed sequence the entries are distinct. Merged row m is held by seq device m // 32; position p belongs to seq device p // 128. The rows of one seq device name at most 13 positions of any one device, and in every packed sequence some device receives exactly 13 rows from every device.
All inputs are finite; a program needn't handle non-finite values.
Results may differ from a plain program's by a relative error of at most 0.0049.
Values may be sent and summed in bfloat16 or wider, within the bound.
A program may use at most 64 MiB of HBM per device.

v0:
```python
import jax
import jax.numpy as jnp
from jax import lax
from jax.sharding import PartitionSpec as P

EPS = 1e-06


def body(attn_mix, resid, out_weight, merger_norm_gain, merger_norm_bias, target, token_grad):
    seq_count = lax.axis_size("seq")
    seq_index = lax.axis_index("seq")
    patches = attn_mix.shape[1]
    width = resid.shape[2]
    merged_rows = patches // 4
    tok_rows = token_grad.shape[1]
    wide = token_grad.shape[2]
    cap = 5 * merged_rows // (3 * seq_count)
    slots_all = seq_count * cap
    routes = target[0].reshape(seq_count, merged_rows)
    owners = routes // tok_rows
    places = routes % tok_rows
    hits = (owners[:, :, None] == jnp.arange(seq_count)[None, None, :]).astype(jnp.int32)
    ranks = jnp.sum((jnp.cumsum(hits, axis=1) - hits) * hits, axis=2)
    column = owners * cap + ranks
    own_column = lax.dynamic_index_in_dim(column, seq_index, 0, keepdims=False)
    pack = (jnp.arange(slots_all)[:, None] == own_column[None, :]).astype(jnp.bfloat16)
    live = (owners == seq_index).reshape(-1)
    source_col = (jnp.arange(seq_count)[:, None] * cap + ranks).reshape(-1)
    row_hot = (
        (places.reshape(-1)[None, :] == jnp.arange(tok_rows)[:, None]) & live[None, :]
    ).astype(jnp.bfloat16)
    col_hot = (source_col[:, None] == jnp.arange(slots_all)[None, :]).astype(jnp.bfloat16)
    place = jnp.dot(row_hot, col_hot, preferred_element_type=jnp.float32).astype(jnp.bfloat16)
    returning = lax.dot_general(
        place, token_grad[0], (((0,), (0,)), ((), ())), preferred_element_type=jnp.float32
    ).astype(jnp.bfloat16)
    returning = returning.reshape(seq_count, cap, wide)
    mixed = attn_mix[0]
    weight = lax.all_gather(out_weight, "dp", axis=0, tiled=True)
    projected = jnp.dot(mixed, weight, preferred_element_type=jnp.float32)
    hidden = resid[0].astype(jnp.float32) + projected
    row_average = jnp.mean(hidden, axis=-1, keepdims=True)
    centered_rows = hidden - row_average
    var = jnp.mean(centered_rows * centered_rows, axis=-1, keepdims=True)
    inverse_deviation = lax.rsqrt(var + EPS)
    standardized_input = centered_rows * inverse_deviation
    normalized_rows = (standardized_input * merger_norm_gain + merger_norm_bias).astype(
        jnp.bfloat16
    )
    merged = normalized_rows.reshape(merged_rows, wide)
    sending = jnp.dot(pack, merged, preferred_element_type=jnp.float32).astype(jnp.bfloat16)
    sending = sending.reshape(seq_count, cap, wide)
    arrived = lax.all_to_all(sending, "seq", split_axis=0, concat_axis=0, tiled=True)
    returned = lax.all_to_all(returning, "seq", split_axis=0, concat_axis=0, tiled=True)
    token_rows = jnp.dot(
        place, arrived.reshape(slots_all, wide), preferred_element_type=jnp.float32
    ).astype(jnp.bfloat16)
    back = lax.dot_general(
        pack,
        returned.reshape(slots_all, wide),
        (((0,), (0,)), ((), ())),
        preferred_element_type=jnp.float32,
    )
    back = back.reshape(patches, width)
    output_gradient = back * merger_norm_gain
    hidden_gradient = inverse_deviation * (
        output_gradient
        - jnp.mean(output_gradient, axis=-1, keepdims=True)
        - standardized_input
        * jnp.mean(output_gradient * standardized_input, axis=-1, keepdims=True)
    )
    rgrad = hidden_gradient.astype(jnp.bfloat16)
    agrad = lax.dot_general(
        rgrad, weight, (((1,), (1,)), ((), ())), preferred_element_type=jnp.float32
    ).astype(jnp.bfloat16)
    return (token_rows[None], rgrad[None], agrad[None])


def solution(mesh):
    placed = (
        P("dp", "seq", None),
        P("dp", "seq", None),
        P("dp", None),
        P(),
        P(),
        P("dp", None),
        P("dp", "seq", None),
    )
    return jax.shard_map(
        body,
        mesh=mesh,
        in_specs=placed,
        out_specs=(P("dp", "seq", None), P("dp", "seq", None), P("dp", "seq", None)),
        check_vma=False,
    )
```

profile of v0, /device:TPU:1, one launch (start us, length us, event | category | flops | bytes accessed | tf_op | source)
XLA Modules:
  0.0 88.0 jit_solution(17168618113230832044)
XLA Ops:
  7.2 0.7 all-gather.2.cloned.1.call-update
  7.9 0.5 broadcast.124
  8.4 1.3 %fusion.15 = (s32[128]{0:T(128)S(1)}, s32[128]{0:T(128)S(1)}) fusion(s32[1,128]{1,0:T(1,128)} %param.12, s32[]{:T(128)} %broadcast.124), kind=kLoop, calls=%fused_computation.44 | loop fusion | flops 1408 | bytes 1540 | tf_op jit(solution)/shard_map/eq | solution.py:30
  10.0 0.2 select_reduce_fusion
  10.4 0.7 compare_bitcast_fusion
  11.1 0.3 convolution_convert_fusion.4
  11.4 0.3 convolution_convert_fusion.1
  11.7 1.0 %reshape.96 = bf16[4,13,5120]{2,1,0:T(8,128)(2,1)} reshape(bf16[52,5120]{1,0:T(8,128)(2,1)S(1)} %convolution_convert_fusion.1) | data formatting | bytes 1064960 | tf_op jit(solution)/shard_map/reshape | solution.py:37
  12.7 4.2 %all-to-all-start.1 = ((bf16[4,13,5120]{2,1,0:T(8,128)(2,1)}), bf16[4,13,5120]{2,1,0:T(8,128)(2,1)S(1)}, u32[]{:S(2)}, u32[]{:S(2)}) async-start(bf16[4,13,5120]{2,1,0:T(8,128)(2,1)} %reshape.96), calls=%async_computation.1 | async-start | bytes 1310720 | tf_op jit(solution)/shard_map/all_to_all | solution.py:54
  17.0 9.1 %all-to-all-done.1 = bf16[4,13,5120]{2,1,0:T(8,128)(2,1)S(1)} async-done(((bf16[4,13,5120]{2,1,0:T(8,128)(2,1)}), bf16[4,13,5120]{2,1,0:T(8,128)(2,1)S(1)}, u32[]{:S(2)}, u32[]{:S(2)}) %all-to-all-start.1) | async-done | bytes 532512 | tf_op jit(solution)/shard_map/all_to_all | solution.py:54
  26.2 0.3 fusion.10
  26.7 29.2 %all-gather.2.cloned.1.call-done = bf16[640,1280]{1,0:T(8,128)(2,1)} async-done(((bf16[80,1280]{1,0:T(8,128)(2,1)}), bf16[640,1280]{1,0:T(8,128)(2,1)}) %all-gather.2.cloned.1.call-update) | async-done | bytes 1638416 | tf_op jit(solution)/shard_map/all_gather | solution.py:39
  55.9 2.0 %fusion.16 = (f32[128]{0:T(128)S(1)}, f32[128,1280]{1,0:T(8,128)S(1)}) fusion(bf16[640,1280]{1,0:T(8,128)(2,1)} %all-gather.2.cloned.1.call-done, bf16[1,128,640]{2,1,0:T(8,128)(2,1)} %param.7, bf16[1,128,1280]{2,1,0:T(8,128)(2,1)S(1)} %copy-done.2), kind=kOutput, calls=%fused_computation.51 | convolution fusion | flops 210206592 | bytes 2785792 | tf_op jit(solution)/shard_map/dot_general | solution.py:40
  58.0 0.2 multiply_reduce_fusion.1
  58.2 0.2 multiply_reduce_fusion.2
  58.7 1.0 %multiply_convert_fusion = (bf16[128,1280]{1,0:T(8,128)(2,1)}, bf16[128,1280]{1,0:T(8,128)(2,1)S(1)}) fusion(f32[128,1280]{1,0:T(8,128)S(1)} %reshape.98, f32[128,1280]{1,0:T(8,128)S(1)} %get-tuple-element.12, f32[128]{0:T(128)S(1)} %get-tuple-element.13, f32[128]{0:T(128)S(1)} %get-tuple-element.14, f32[1280]{0:T(1024)S(1)} %copy-done.3, ...), kind=kLoop, calls=%fused_computation.9 | loop fusion | flops 1802240 | bytes 1978368 | tf_op jit(solution)/shard_map/convert_element_type | solution.py:72
  59.7 0.9 %reshape.93 = bf16[32,5120]{1,0:T(8,128)(2,1)} reshape(bf16[128,1280]{1,0:T(8,128)(2,1)S(1)} %get-tuple-element.6) | data formatting | bytes 655360 | tf_op jit(solution)/shard_map/reshape | solution.py:50
  60.6 1.4 %convolution_convert_fusion.2 = bf16[52,5120]{1,0:T(8,128)(2,1)S(1)} fusion(bf16[32,5120]{1,0:T(8,128)(2,1)} %reshape.93, s32[32]{0:T(128)S(1)} %dynamic-slice_bitcast_fusion), kind=kOutput, calls=%fused_computation.3 | convolution fusion | flops 17307264 | bytes 860288 | tf_op jit(solution)/shard_map/dot_general | solution.py:51
  62.0 1.0 %reshape.94 = bf16[4,13,5120]{2,1,0:T(8,128)(2,1)} reshape(bf16[52,5120]{1,0:T(8,128)(2,1)S(1)} %convolution_convert_fusion.2) | data formatting | bytes 1064960 | tf_op jit(solution)/shard_map/reshape | solution.py:52
  63.0 5.9 %all-to-all-start = ((bf16[4,13,5120]{2,1,0:T(8,128)(2,1)}), bf16[4,13,5120]{2,1,0:T(8,128)(2,1)}, u32[]{:S(2)}, u32[]{:S(2)}) async-start(bf16[4,13,5120]{2,1,0:T(8,128)(2,1)} %reshape.94), calls=%async_computation | async-start | bytes 1310720 | tf_op jit(solution)/shard_map/all_to_all | solution.py:53
  69.0 2.3 %fusion.2 = bf16[1,128,640]{2,1,0:T(8,128)(2,1)} fusion(bf16[128,1280]{1,0:T(8,128)(2,1)} %get-tuple-element.5, bf16[640,1280]{1,0:T(8,128)(2,1)S(1)} %copy-done.1), kind=kOutput, calls=%fused_computation.7 | convolution fusion | flops 209797120 | bytes 2129920 | tf_op jit(solution)/shard_map/dot_general | solution.py:73
  71.2 7.1 %all-to-all-done = bf16[4,13,5120]{2,1,0:T(8,128)(2,1)} async-done(((bf16[4,13,5120]{2,1,0:T(8,128)(2,1)}), bf16[4,13,5120]{2,1,0:T(8,128)(2,1)}, u32[]{:S(2)}, u32[]{:S(2)}) %all-to-all-start) | async-done | bytes 532512 | tf_op jit(solution)/shard_map/all_to_all | solution.py:53
  78.3 1.3 %reshape.95 = bf16[52,5120]{1,0:T(8,128)(2,1)S(1)} reshape(bf16[4,13,5120]{2,1,0:T(8,128)(2,1)} %all-to-all-done) | data formatting | bytes 1064960 | tf_op jit(solution)/shard_map/reshape | solution.py:56
  79.6 1.6 %fusion = bf16[1,128,5120]{2,1,0:T(8,128)(2,1)} fusion(bf16[128,52]{0,1:T(8,128)(2,1)S(1)} %convolution_convert_fusion.4, bf16[52,5120]{1,0:T(8,128)(2,1)S(1)} %reshape.95), kind=kOutput, calls=%fused_computation.1 | convolution fusion | flops 68812800 | bytes 1856512 | tf_op jit(solution)/shard_map/dot_general | solution.py:55
  (24 shorter events, 1.1 us)
Async XLA Ops:
  7.2 4.2 %copy-start = (bf16[1,128,5120]{2,1,0:T(8,128)(2,1)S(1)}, bf16[1,128,5120]{2,1,0:T(8,128)(2,1)}, u32[]{:S(2)}) copy-start(bf16[1,128,5120]{2,1,0:T(8,128)(2,1)} %param.13) | copy-start | bytes 3932164
  7.2 48.8 %all-gather.2.cloned.1.call-start = ((), (), s32[]{:S(2)}) async-start(), calls=%async_computation.2 | async-start | bytes 1843200 | tf_op jit(solution)/shard_map/all_gather | solution.py:39
  12.7 13.3 %all-to-all-start.1 = ((bf16[4,13,5120]{2,1,0:T(8,128)(2,1)}), bf16[4,13,5120]{2,1,0:T(8,128)(2,1)S(1)}, u32[]{:S(2)}, u32[]{:S(2)}) async-start(bf16[4,13,5120]{2,1,0:T(8,128)(2,1)} %reshape.96), calls=%async_computation.1 | async-start | bytes 1310720 | tf_op jit(solution)/shard_map/all_to_all | solution.py:54
  17.0 39.0 %copy-start.2 = (bf16[1,128,1280]{2,1,0:T(8,128)(2,1)S(1)}, bf16[1,128,1280]{2,1,0:T(8,128)(2,1)}, u32[]{:S(2)}) copy-start(bf16[1,128,1280]{2,1,0:T(8,128)(2,1)} %param.8) | copy-start | bytes 983044
  26.7 31.5 %copy-start.3 = (f32[1280]{0:T(1024)S(1)}, f32[1280]{0:T(1024)}, u32[]{:S(2)}) copy-start(f32[1280]{0:T(1024)} %param.10) | copy-start | bytes 15364
  58.0 0.7 copy-start.4
  60.6 8.3 %copy-start.1 = (bf16[640,1280]{1,0:T(8,128)(2,1)S(1)}, bf16[640,1280]{1,0:T(8,128)(2,1)}, u32[]{:S(2)}) copy-start(bf16[640,1280]{1,0:T(8,128)(2,1)} %all-gather.2.cloned.1.call-done) | copy-start | bytes 4915204
  63.0 15.3 %all-to-all-start = ((bf16[4,13,5120]{2,1,0:T(8,128)(2,1)}), bf16[4,13,5120]{2,1,0:T(8,128)(2,1)}, u32[]{:S(2)}, u32[]{:S(2)}) async-start(bf16[4,13,5120]{2,1,0:T(8,128)(2,1)} %reshape.94), calls=%async_computation | async-start | bytes 1310720 | tf_op jit(solution)/shard_map/all_to_all | solution.py:53
Sparse Core Ops, SparseCore 0:
  10.2 45.7 all-gather.1
where the time goes:
time: 89.4 us; the launch traced here: 88 us
  waiting for transfers between devices  46 us (51%)
  between operations  14.1 us (16%)
  starting transfers between devices  10.2 us (11%)
  matrix products  8.17 us (9%)
  local copies, waits for them, and re-layouts  5.52 us (6%)
  other arithmetic  3.95 us (4%)
    all_gather x1, waiting for transfers between devices, body(): weight = lax.all_gather(out_weight, 'dp', axis=0, tiled=True)  29.2 us
    all_to_all x1, waiting for transfers between devices, body(): lax.all_to_all(returning, 'seq', split_axis=0, concat_axis=0, tiled=True)  9.06 us
    all_to_all x1, waiting for transfers between devices, body(): lax.all_to_all(sending, 'seq', split_axis=0, concat_axis=0, tiled=True)  7.08 us
    all_to_all x1, starting transfers between devices, body(): lax.all_to_all(sending, 'seq', split_axis=0, concat_axis=0, tiled=True)  5.91 us
    all_to_all x1, starting transfers between devices, body(): lax.all_to_all(returning, 'seq', split_axis=0, concat_axis=0, tiled=True)  4.25 us
    dot_general x1, matrix products, body(): lax.dot_general(rgrad, weight, (((1,), (1,)), ((), ())), preferred_elemen...  2.27 us
    dot_general x1, matrix products, body(): projected = jnp.dot(mixed, weight, preferred_element_type=jnp.float32)  2.04 us
  transfers between devices with their start and end apart: 3, of which 3 were waited for; matrix products, arithmetic and copies ran while one was open for 9% of the time, Pallas kernels for 0%

commit v1 on v0

v1 whole, which is shorter than its diff:
```python
import functools
import math

import jax
import jax.numpy as jnp
from jax import lax
from jax.experimental import pallas as pl
from jax.experimental.pallas import tpu as pltpu
from jax.sharding import PartitionSpec as P

EPS = 1e-06
F32 = jnp.float32
BF16 = jnp.bfloat16
MESH = pl.DeviceIdType.MESH


def iota(shape, axis):
    return lax.broadcasted_iota(jnp.int32, shape, axis)


def remote(src, dst, send, recv, device):
    return pltpu.make_async_remote_copy(
        src_ref=src, dst_ref=dst, send_sem=send, recv_sem=recv,
        device_id=device, device_id_type=MESH,
    )


def kernel(dims, mix_hbm, resid_hbm, w_hbm, gain_ref, bias_ref, target_ref, tg_hbm,
           rows_hbm, rgrad_hbm, agrad_hbm,
           mix, resid, tg, wbuf, bsend, brecv, fsend, frecv, xhat_s, rows_s, rgrad_s, agrad_s,
           load_sem, own_sem, zsend, ysend, psend, wrecv, precv, bs_sem, br_sem, fs_sem, fr_sem,
           out_sem):
    S, D, A, B, cap, R, wcuts, fcuts = dims
    n_tok, wide = tg.shape
    patches, width = resid.shape
    M = target_ref.shape[1]
    merged = M // S
    group = patches // merged
    half = width // 2
    depth = wbuf.shape[2]
    SR = S * R
    me = lax.axis_index("seq")
    d = lax.axis_index("dp")
    a, b = d // B, d % B
    h = me % 2
    partner = me + 1 - 2 * h

    loads = [
        pltpu.make_async_copy(w_hbm.at[:, i * half:(i + 1) * half], wbuf.at[i, d], own_sem.at[i])
        for i in range(2)
    ]
    tg_load = pltpu.make_async_copy(tg_hbm.at[0], tg, load_sem.at[0])
    mix_load = pltpu.make_async_copy(mix_hbm.at[0], mix, load_sem.at[1])
    resid_load = pltpu.make_async_copy(resid_hbm.at[0], resid, load_sem.at[2])
    for c in loads + [tg_load, mix_load, resid_load]:
        c.start()

    barrier = pltpu.get_barrier_semaphore()
    for r in range(1, S):
        pl.semaphore_signal(barrier, inc=1, device_id={"seq": lax.rem(me + r, S)}, device_id_type=MESH)
    for r in range(1, B):
        pl.semaphore_signal(barrier, inc=1, device_id={"dp": a * B + lax.rem(b + r, B)}, device_id_type=MESH)

    @pl.when(a > 0)
    def _():
        pl.semaphore_signal(barrier, inc=1, device_id={"dp": d - B}, device_id_type=MESH)

    @pl.when(a < A - 1)
    def _():
        pl.semaphore_signal(barrier, inc=1, device_id={"dp": d + B}, device_id_type=MESH)

    for c in loads:
        c.wait()
    ends = jnp.where(a > 0, 1, 0) + jnp.where(a < A - 1, 1, 0)
    pl.semaphore_wait(barrier, S - 1 + B - 1 + ends)

    nc = len(wcuts)

    def piece(half_index, shard, c):
        lo, hi = wcuts[c]
        return wbuf.at[half_index, shard, :, lo:hi]

    def z_copy(src_a, side, k, c):
        p = piece(h, src_a * B + b, c)
        return remote(p, p, zsend.at[0 if side > 0 else 1, k, c],
                      wrecv.at[src_a * B + b, c], {"dp": d - side * B})

    def y_copy(src_a, r, c):
        p = piece(h, src_a * B + b, c)
        return remote(p, p, ysend.at[src_a, r - 1, c], wrecv.at[src_a * B + b, c],
                      {"dp": a * B + lax.rem(b + r, B)})

    def p_copy(shard, c):
        p = piece(h, shard, c)
        return remote(p, p, psend.at[shard, c], precv.at[shard, c], {"seq": partner})

    def arrived(shard, c):
        p = piece(h, shard, c)
        remote(p, p, psend.at[shard, c], wrecv.at[shard, c], {"seq": partner}).wait_recv()

    def each_z(k, side, act):
        src = a + side * k
        ok = jnp.logical_and(src >= 0, src < A)
        onward = jnp.logical_and(a - side >= 0, a - side < A)

        @pl.when(jnp.logical_and(ok, onward))
        def _():
            act(src)

    for c in range(nc):
        for side in (1, -1):
            each_z(0, side, lambda src, side=side, c=c: z_copy(src, side, 0, c).start())
        for r in range(1, B):
            y_copy(a, r, c).start()

    t_row = target_ref[...].astype(F32)
    diag = iota((M, M), 0) == iota((M, M), 1)
    t_col = jnp.sum(jnp.where(diag, jnp.broadcast_to(t_row, (M, M)), 0.0), axis=1, keepdims=True)

    def bucket(v, size):
        out = jnp.zeros(v.shape, F32)
        for o in range(1, S):
            out = out + jnp.where(v >= float(o * size), 1.0, 0.0)
        return out

    own_row, own_col = bucket(t_row, n_tok), bucket(t_col, n_tok)
    place_col = t_col - own_col * n_tok
    m_row, m_col = iota((1, M), 1).astype(F32), iota((M, 1), 0).astype(F32)
    blk_row, blk_col = bucket(m_row, merged), bucket(m_col, merged)
    same = (own_col == own_row) & (blk_col == blk_row) & (m_row < m_col)
    rank_col = jnp.sum(jnp.where(same, 1.0, 0.0), axis=1, keepdims=True)
    me_f = me.astype(F32)

    def relative(v):
        u = v - me_f
        return jnp.where(u < 0.0, u + float(S), u)

    tok_row = iota((1, n_tok), 1).astype(F32)
    hit = (place_col == tok_row) & (own_col == me_f)
    st_row = jnp.sum(jnp.where(hit, relative(blk_col) * R + rank_col + 1.0, 0.0), axis=0, keepdims=True)
    st_row = jnp.where(st_row > 0.0, st_row - 1.0, -4.0 * SR)
    slot_col = iota((SR, 1), 0).astype(F32)
    take = jnp.concatenate(
        [jnp.where(slot_col == st_row + float(j * cap), 1.0, 0.0).astype(BF16) for j in range(group)], axis=1
    )
    tg_load.wait()
    stacked = jnp.concatenate([tg[:, j * width:(j + 1) * width] for j in range(group)], axis=0)
    back_rows = jnp.dot(take, stacked, preferred_element_type=F32)
    back_rows = back_rows.reshape(S, R // 8, 8, width).astype(BF16)
    brecv[0] = back_rows[0]
    bsend[...] = back_rows[1:]

    def b_copy(r):
        return remote(bsend.at[r - 1], brecv.at[S - r], bs_sem.at[r - 1], br_sem.at[S - r - 1],
                      {"seq": lax.rem(me + r, S)})

    for r in range(1, S):
        b_copy(r).start()

    p_int = iota((1, patches), 1)
    p_blk = jnp.zeros((1, patches), F32)
    for o in range(1, merged):
        p_blk = p_blk + jnp.where(p_int >= o * group, 1.0, 0.0)
    p_sub = p_int.astype(F32) - p_blk * group
    mine = m_col == p_blk + me_f * merged
    ps_row = jnp.sum(jnp.where(mine, relative(own_col) * R + rank_col, 0.0), axis=0, keepdims=True)
    ps_row = ps_row + p_sub * cap
    pack = jnp.where(slot_col == ps_row, 1.0, 0.0).astype(BF16)
    p_diag = iota((patches, patches), 0) == iota((patches, patches), 1)
    ps_col = jnp.sum(jnp.where(p_diag, jnp.broadcast_to(ps_row, (patches, patches)), 0.0), axis=1, keepdims=True)
    slot_row = iota((1, SR), 1).astype(F32)
    unpack = jnp.where(ps_col == slot_row, 1.0, 0.0).astype(BF16)
    t_diag = iota((n_tok, n_tok), 0) == iota((n_tok, n_tok), 1)
    st_col = jnp.sum(jnp.where(t_diag, jnp.broadcast_to(st_row, (n_tok, n_tok)), 0.0), axis=1, keepdims=True)
    put = jnp.concatenate(
        [jnp.where(st_col + float(j * cap) == slot_row, 1.0, 0.0).astype(BF16) for j in range(group)], axis=0
    )

    def y_arrivals(k):
        for c in range(nc):
            for side in ((1,) if k == 0 else (1, -1)):
                src = a + side * k

                @pl.when(jnp.logical_and(src >= 0, src < A))
                def _(src=src, c=c):
                    for r in range(1, B):
                        shard = src * B + lax.rem(b + r, B)
                        arrived(shard, c)
                        p_copy(shard, c).start()

    for k in range(1, A):
        for c in range(nc):
            for side in (1, -1):
                src = a + side * k

                @pl.when(jnp.logical_and(src >= 0, src < A))
                def _(src=src, side=side, k=k, c=c):
                    arrived(src * B + b, c)
                    for r in range(1, B):
                        y_copy(src, r, c).start()
                    if k < A - 1:
                        each_z(k, side, lambda s: z_copy(s, side, k, c).start())
                    p_copy(src * B + b, c).start()
        y_arrivals(k - 1)
    y_arrivals(A - 1)

    def other_shards(act):
        @pl.loop(0, D)
        def _(shard):
            @pl.when(shard != d)
            def _():
                for c in range(nc):
                    act(shard, c)

    def p_wait(shard, c):
        p = piece(1 - h, shard, c)
        remote(p, p, psend.at[shard, c], precv.at[shard, c], {"seq": partner}).wait_recv()

    other_shards(p_wait)

    def weight(i):
        if depth % 16 == 0:
            return wbuf[i].reshape(D * depth, half)
        return jnp.concatenate([wbuf[i, s].astype(F32) for s in range(D)], axis=0).astype(BF16)

    mix_load.wait()
    resid_load.wait()
    w = [weight(i) for i in range(2)]
    hidden = resid[...].astype(F32) + jnp.concatenate(
        [jnp.dot(mix[...], w[i], preferred_element_type=F32) for i in range(2)], axis=1
    )
    centered = hidden - jnp.mean(hidden, axis=-1, keepdims=True)
    rstd = lax.rsqrt(jnp.mean(centered * centered, axis=-1, keepdims=True) + EPS)
    xhat = centered * rstd
    xhat_s[...] = xhat
    normed = (xhat * gain_ref[...] + bias_ref[...]).astype(BF16)

    def f_copy(c, r):
        lo, hi = fcuts[c]
        return remote(fsend.at[r - 1, :, :, lo:hi], frecv.at[S - r, :, :, lo:hi],
                      fs_sem.at[c, r - 1], fr_sem.at[c, S - r - 1], {"seq": lax.rem(me + r, S)})

    for c, (lo, hi) in enumerate(fcuts):
        out = jnp.dot(pack, normed[:, lo:hi], preferred_element_type=F32)
        out = out.reshape(S, R // 8, 8, hi - lo).astype(BF16)
        frecv[0, :, :, lo:hi] = out[0]
        fsend[:, :, :, lo:hi] = out[1:]
        for r in range(1, S):
            f_copy(c, r).start()

    for r in range(1, S):
        b_copy(S - r).wait_recv()
    returned = brecv[...].astype(F32).reshape(SR, width).astype(BF16)
    gy = jnp.dot(unpack, returned, preferred_element_type=F32) * gain_ref[...]
    xh = xhat_s[...]
    hg = rstd * (gy - jnp.mean(gy, axis=-1, keepdims=True) - xh * jnp.mean(gy * xh, axis=-1, keepdims=True))
    rgrad = hg.astype(BF16)
    rgrad_s[...] = rgrad
    rg_out = pltpu.make_async_copy(rgrad_s, rgrad_hbm.at[0], out_sem.at[0])
    rg_out.start()
    agrad = sum(
        lax.dot_general(rgrad[:, i * half:(i + 1) * half], w[i], (((1,), (1,)), ((), ())),
                        preferred_element_type=F32)
        for i in range(2)
    )
    agrad_s[...] = agrad.astype(BF16)
    ag_out = pltpu.make_async_copy(agrad_s, agrad_hbm.at[0], out_sem.at[1])
    ag_out.start()

    outs = [rg_out, ag_out]
    for c, (lo, hi) in enumerate(fcuts):
        for r in range(1, S):
            f_copy(c, S - r).wait_recv()
        got = frecv[:, :, :, lo:hi].astype(F32).reshape(SR, hi - lo).astype(BF16)
        placed = jnp.dot(put, got, preferred_element_type=F32).astype(BF16)
        for j in range(group):
            part = (slice(None), slice(j * width + lo, j * width + hi))
            rows_s[part] = placed[j * n_tok:(j + 1) * n_tok]
            copy = pltpu.make_async_copy(rows_s.at[part], rows_hbm.at[(0,) + part],
                                         out_sem.at[2 + c * group + j])
            copy.start()
            outs.append(copy)

    for c in range(nc):
        for side in (1, -1):
            for k in range(A - 1):
                each_z(k, side, lambda src, side=side, k=k, c=c: z_copy(src, side, k, c).wait_send())
        for src in range(A):
            for r in range(1, B):
                y_copy(src, r, c).wait_send()
    other_shards(lambda shard, c: p_copy(shard, c).wait_send())
    for r in range(1, S):
        b_copy(r).wait_send()
        for c in range(len(fcuts)):
            f_copy(c, r).wait_send()
    for copy in outs:
        copy.wait()


def cuts(total, parts):
    lanes = total // 128
    edges = [128 * (lanes * i // parts) for i in range(parts)] + [total]
    return tuple((edges[i], edges[i + 1]) for i in range(parts))


def body(S, D, attn_mix, resid, out_weight, gain, bias, target, token_grad):
    patches, columns = attn_mix.shape[1:]
    width = resid.shape[2]
    n_tok, wide = token_grad.shape[1:]
    merged = target.shape[1] // S
    group = patches // merged
    cap = 5 * merged // (3 * S)
    R = -(-group * cap // 8) * 8
    B = 2 ** int(math.log2(D) // 2)
    A = D // B
    depth = out_weight.shape[0]
    wcuts = cuts(width // 2, 2)
    fcuts = cuts(width, 5)
    nc, nf = len(wcuts), len(fcuts)
    dims = (S, D, A, B, cap, R, wcuts, fcuts)
    hbm = pl.BlockSpec(memory_space=pl.ANY)
    vmem = pl.BlockSpec(memory_space=pltpu.VMEM)
    dma = pltpu.SemaphoreType.DMA
    return pl.pallas_call(
        functools.partial(kernel, dims),
        out_shape=(
            jax.ShapeDtypeStruct(token_grad.shape, BF16),
            jax.ShapeDtypeStruct(resid.shape, BF16),
            jax.ShapeDtypeStruct(attn_mix.shape, BF16),
        ),
        in_specs=[hbm, hbm, hbm, vmem, vmem, vmem, hbm],
        out_specs=(hbm, hbm, hbm),
        scratch_shapes=[
            pltpu.VMEM((patches, columns), BF16),
            pltpu.VMEM((patches, width), BF16),
            pltpu.VMEM((n_tok, wide), BF16),
            pltpu.VMEM((2, D, depth, width // 2), BF16),
            pltpu.VMEM((S - 1, R // 8, 8, width), BF16),
            pltpu.VMEM((S, R // 8, 8, width), BF16),
            pltpu.VMEM((S - 1, R // 8, 8, width), BF16),
            pltpu.VMEM((S, R // 8, 8, width), BF16),
            pltpu.VMEM((patches, width), F32),
            pltpu.VMEM((n_tok, wide), BF16),
            pltpu.VMEM((patches, width), BF16),
            pltpu.VMEM((patches, columns), BF16),
            dma((3,)), dma((2,)), dma((2, A - 1, nc)), dma((A, B - 1, nc)), dma((D, nc)),
            dma((D, nc)), dma((D, nc)), dma((S - 1,)), dma((S - 1,)), dma((nf, S - 1)),
            dma((nf, S - 1)), dma((2 + nf * group,)),
        ],
        compiler_params=pltpu.CompilerParams(
            collective_id=0, has_side_effects=True, vmem_limit_bytes=60 * 1024 * 1024
        ),
    )(attn_mix, resid, out_weight, gain[None], bias[None], target, token_grad)


def solution(mesh):
    placed = (
        P("dp", "seq", None),
        P("dp", "seq", None),
        P("dp", None),
        P(),
        P(),
        P("dp", None),
        P("dp", "seq", None),
    )
    return jax.shard_map(
        functools.partial(body, mesh.shape["seq"], mesh.shape["dp"]),
        mesh=mesh,
        in_specs=placed,
        out_specs=(P("dp", "seq", None), P("dp", "seq", None), P("dp", "seq", None)),
        check_vma=False,
    )
```

time: 89.4 us -> 38.7 us (0.43)
  waiting for transfers between devices: 46 us -> 0 us
  Pallas kernels: 0 us -> 30.9 us
  between operations: 14.1 us -> 0.66 us
  starting transfers between devices: 10.2 us -> 0 us
  matrix products: 8.17 us -> 0 us
  other arithmetic: 3.95 us -> 0 us
  local copies, waits for them, and re-layouts: 5.52 us -> 6.5 us
    pallas_call x0 -> x1, Pallas kernels: none -> 30.9 us  [body(): pl.pallas_call(functools.partial(kernel, dims), out_shape=(jax.ShapeDtype...]
    all_gather x1 -> x0, waiting for transfers between devices: 29.2 us -> none  [body(): weight = lax.all_gather(out_weight, 'dp', axis=0, tiled=True)]
    all_to_all x2 -> x0, waiting for transfers between devices: 16.1 us -> none  [the longest x1 9.06 us: body(): lax.all_to_all(returning, 'seq', split_axis=0, concat_axis=0, tiled=True)]
    all_to_all x2 -> x0, starting transfers between devices: 10.2 us -> none  [the longest x1 5.91 us: body(): lax.all_to_all(sending, 'seq', split_axis=0, concat_axis=0, tiled=True)]
    dot_general x7 -> x0, matrix products: 8.17 us -> none  [the longest x1 2.27 us: body(): lax.dot_general(rgrad, weight, (((1,), (1,)), ((), ())), preferred_elemen...]
    reshape x6 -> x0, local copies, waits for them, and re-layouts: 4.6 us -> none  [the longest x1 1.27 us: body(): arrived.reshape(slots_all, wide)]
    unnamed x11 -> x7, local copies, waits for them, and re-layouts: 0.74 us -> 3.91 us
    broadcast_in_dim x0 -> x2, local copies, waits for them, and re-layouts: none -> 2.59 us  [the longest x1 1.29 us: body(): gain[None]]
  transfers between devices with their start and end apart: 3 -> 0, of which waited for: 3 -> 0; matrix products, arithmetic and copies ran while one was open for 9% -> 0% of each run, Pallas kernels for 0% -> 0%
where the time goes in v1:
time: 38.7 us; the launch traced here: 38 us
  Pallas kernels  30.9 us (80%)
  local copies, waits for them, and re-layouts  6.5 us (17%)
  between operations  0.66 us (2%)
    pallas_call x1, Pallas kernels, body(): pl.pallas_call(functools.partial(kernel, dims), out_shape=(jax.ShapeDtype...  30.9 us
    unnamed x7, local copies, waits for them, and re-layouts  3.91 us
    broadcast_in_dim x1, local copies, waits for them, and re-layouts, body(): gain[None]  1.29 us
    broadcast_in_dim x1, local copies, waits for them, and re-layouts, body(): bias[None]  1.29 us

profile of v1, /device:TPU:1, one launch (start us, length us, event | category | flops | bytes accessed | tf_op | source)
XLA Modules:
  0.0 38.0 jit_solution(10814157153577196259)
XLA Ops:
  0.6 1.3 %broadcast_in_dim.6.gain_ref = f32[1,1280]{1,0:T(1,128)} reshape(f32[1280]{0:T(1024)} %param.10) | data formatting | bytes 10240 | tf_op jit(solution)/shard_map/broadcast_in_dim | solution.py:353
  1.9 1.3 %broadcast_in_dim.7.bias_ref = f32[1,1280]{1,0:T(1,128)} reshape(f32[1280]{0:T(1024)} %param.11) | data formatting | bytes 10240 | tf_op jit(solution)/shard_map/broadcast_in_dim | solution.py:353
  3.2 30.9 %shard_map.94 = (bf16[1,128,5120]{2,1,0:T(8,128)(2,1)}, bf16[1,128,1280]{2,1,0:T(8,128)(2,1)}, bf16[1,128,640]{2,1,0:T(8,128)(2,1)}) custom-call(bf16[1,128,640]{2,1,0:T(8,128)(2,1)} %mix_hbm.1, bf16[1,128,1280]{2,1,0:T(8,128)(2,1)} %resid_hbm.1, bf16[80,1280]{1,0:T(8,128)(2,1)} %w_hbm.1, f32[1,1280]{1,0:T(1,128)} %broadcast_in_dim.6.gain_ref, ...), custom_call_target="tpu_custom_call" | custom-call | tf_op jit(solution)/shard_map/pallas_call | solution.py:324
  34.1 0.0 copy-start
  34.1 0.0 copy-start.1
  34.1 2.5 %copy.13 = bf16[1,128,5120]{2,1,0:T(8,128)(2,1)} copy(bf16[1,128,5120]{2,1,0:T(8,128)(2,1)} %get-tuple-element.6) | data formatting | bytes 2621440
  36.7 0.0 copy-done
  36.7 0.7 %copy.14 = bf16[1,128,1280]{2,1,0:T(8,128)(2,1)} copy(bf16[1,128,1280]{2,1,0:T(8,128)(2,1)S(1)} %copy-done) | data formatting | bytes 655360
  37.4 0.0 copy-done.1
  37.4 0.7 %copy.15 = bf16[1,128,640]{2,1,0:T(8,128)(2,1)} copy(bf16[1,128,640]{2,1,0:T(8,128)(2,1)S(1)} %copy-done.1) | data formatting | bytes 327680
Async XLA Ops:
  34.1 2.5 %copy-start = (bf16[1,128,1280]{2,1,0:T(8,128)(2,1)S(1)}, bf16[1,128,1280]{2,1,0:T(8,128)(2,1)}, u32[]{:S(2)}) copy-start(bf16[1,128,1280]{2,1,0:T(8,128)(2,1)} %get-tuple-element.7) | copy-start | bytes 983044
  34.1 3.3 %copy-start.1 = (bf16[1,128,640]{2,1,0:T(8,128)(2,1)S(1)}, bf16[1,128,640]{2,1,0:T(8,128)(2,1)}, u32[]{:S(2)}) copy-start(bf16[1,128,640]{2,1,0:T(8,128)(2,1)} %get-tuple-element.8) | copy-start | bytes 491524

commit v2 on v1

--- a/solution.py
+++ b/solution.py
@@ -26,12 +26,13 @@
 
 
 def kernel(dims, mix_hbm, resid_hbm, w_hbm, gain_ref, bias_ref, target_ref, tg_hbm,
-           rows_hbm, rgrad_hbm, agrad_hbm,
-           mix, resid, tg, wbuf, bsend, brecv, fsend, frecv, xhat_s, rows_s, rgrad_s, agrad_s,
-           load_sem, own_sem, zsend, ysend, psend, wrecv, precv, bs_sem, br_sem, fs_sem, fr_sem,
-           out_sem):
+           rows_s, rgrad_s, agrad_s,
+           mix, resid, tg, wbuf, bsend, brecv, fsend, frecv, xhat_s,
+           load_sem, own_sem, zsend, ysend, psend, wrecv, precv, bs_sem, br_sem, fs_sem, fr_sem):
     S, D, A, B, cap, R, wcuts, fcuts = dims
     n_tok, wide = tg.shape
+    gain = gain_ref[...].reshape(1, -1)
+    bias = bias_ref[...].reshape(1, -1)
     patches, width = resid.shape
     M = target_ref.shape[1]
     merged = M // S
@@ -233,7 +234,7 @@
     rstd = lax.rsqrt(jnp.mean(centered * centered, axis=-1, keepdims=True) + EPS)
     xhat = centered * rstd
     xhat_s[...] = xhat
-    normed = (xhat * gain_ref[...] + bias_ref[...]).astype(BF16)
+    normed = (xhat * gain + bias).astype(BF16)
 
     def f_copy(c, r):
         lo, hi = fcuts[c]
@@ -251,23 +252,18 @@
     for r in range(1, S):
         b_copy(S - r).wait_recv()
     returned = brecv[...].astype(F32).reshape(SR, width).astype(BF16)
-    gy = jnp.dot(unpack, returned, preferred_element_type=F32) * gain_ref[...]
+    gy = jnp.dot(unpack, returned, preferred_element_type=F32) * gain
     xh = xhat_s[...]
     hg = rstd * (gy - jnp.mean(gy, axis=-1, keepdims=True) - xh * jnp.mean(gy * xh, axis=-1, keepdims=True))
     rgrad = hg.astype(BF16)
-    rgrad_s[...] = rgrad
-    rg_out = pltpu.make_async_copy(rgrad_s, rgrad_hbm.at[0], out_sem.at[0])
-    rg_out.start()
+    rgrad_s[0] = rgrad
     agrad = sum(
         lax.dot_general(rgrad[:, i * half:(i + 1) * half], w[i], (((1,), (1,)), ((), ())),
                         preferred_element_type=F32)
         for i in range(2)
     )
-    agrad_s[...] = agrad.astype(BF16)
-    ag_out = pltpu.make_async_copy(agrad_s, agrad_hbm.at[0], out_sem.at[1])
-    ag_out.start()
-
-    outs = [rg_out, ag_out]
+    agrad_s[0] = agrad.astype(BF16)
+
     for c, (lo, hi) in enumerate(fcuts):
         for r in range(1, S):
             f_copy(c, S - r).wait_recv()
@@ -275,11 +271,7 @@
         placed = jnp.dot(put, got, preferred_element_type=F32).astype(BF16)
         for j in range(group):
             part = (slice(None), slice(j * width + lo, j * width + hi))
-            rows_s[part] = placed[j * n_tok:(j + 1) * n_tok]
-            copy = pltpu.make_async_copy(rows_s.at[part], rows_hbm.at[(0,) + part],
-                                         out_sem.at[2 + c * group + j])
-            copy.start()
-            outs.append(copy)
+            rows_s[(0,) + part] = placed[j * n_tok:(j + 1) * n_tok]
 
     for c in range(nc):
         for side in (1, -1):
@@ -293,7 +285,14 @@
         b_copy(r).wait_send()
         for c in range(len(fcuts)):
             f_copy(c, r).wait_send()
-    for copy in outs:
+
+
+def write_out(a_ref, b_ref, c_ref, a_hbm, b_hbm, c_hbm, sems):
+    pairs = ((a_ref, a_hbm), (b_ref, b_hbm), (c_ref, c_hbm))
+    copies = [pltpu.make_async_copy(src, dst, sems.at[i]) for i, (src, dst) in enumerate(pairs)]
+    for copy in copies:
+        copy.start()
+    for copy in copies:
         copy.wait()
 
 
@@ -318,18 +317,20 @@
     fcuts = cuts(width, 5)
     nc, nf = len(wcuts), len(fcuts)
     dims = (S, D, A, B, cap, R, wcuts, fcuts)
-    hbm = pl.BlockSpec(memory_space=pl.ANY)
+    hbm = pl.BlockSpec(memory_space=pltpu.HBM)
     vmem = pl.BlockSpec(memory_space=pltpu.VMEM)
     dma = pltpu.SemaphoreType.DMA
-    return pl.pallas_call(
+    result_bytes = 2 * (token_grad.size + resid.size + attn_mix.size)
+    grant = 60 * 1024 * 1024 - result_bytes - 320 * 1024
+    outs = pl.pallas_call(
         functools.partial(kernel, dims),
         out_shape=(
-            jax.ShapeDtypeStruct(token_grad.shape, BF16),
-            jax.ShapeDtypeStruct(resid.shape, BF16),
-            jax.ShapeDtypeStruct(attn_mix.shape, BF16),
+            pltpu.VMEM(token_grad.shape, BF16),
+            pltpu.VMEM(resid.shape, BF16),
+            pltpu.VMEM(attn_mix.shape, BF16),
         ),
         in_specs=[hbm, hbm, hbm, vmem, vmem, vmem, hbm],
-        out_specs=(hbm, hbm, hbm),
+        out_specs=(vmem, vmem, vmem),
         scratch_shapes=[
             pltpu.VMEM((patches, columns), BF16),
             pltpu.VMEM((patches, width), BF16),
@@ -340,17 +341,22 @@
             pltpu.VMEM((S - 1, R // 8, 8, width), BF16),
             pltpu.VMEM((S, R // 8, 8, width), BF16),
             pltpu.VMEM((patches, width), F32),
-            pltpu.VMEM((n_tok, wide), BF16),
-            pltpu.VMEM((patches, width), BF16),
-            pltpu.VMEM((patches, columns), BF16),
             dma((3,)), dma((2,)), dma((2, A - 1, nc)), dma((A, B - 1, nc)), dma((D, nc)),
             dma((D, nc)), dma((D, nc)), dma((S - 1,)), dma((S - 1,)), dma((nf, S - 1)),
-            dma((nf, S - 1)), dma((2 + nf * group,)),
+            dma((nf, S - 1)),
         ],
         compiler_params=pltpu.CompilerParams(
-            collective_id=0, has_side_effects=True, vmem_limit_bytes=60 * 1024 * 1024
+            collective_id=0, has_side_effects=True, vmem_limit_bytes=grant
         ),
-    )(attn_mix, resid, out_weight, gain[None], bias[None], target, token_grad)
+    )(attn_mix, resid, out_weight, gain, bias, target, token_grad)
+    return pl.pallas_call(
+        write_out,
+        out_shape=tuple(jax.ShapeDtypeStruct(o.shape, o.dtype) for o in outs),
+        in_specs=[vmem] * 3,
+        out_specs=(hbm,) * 3,
+        scratch_shapes=[dma((3,))],
+        compiler_params=pltpu.CompilerParams(vmem_limit_bytes=8 * 1024 * 1024),
+    )(*outs)
 
 
 def solution(mesh):

time: 38.7 us -> 32.6 us (0.84)
  local copies, waits for them, and re-layouts: 6.5 us -> 0 us
  Pallas kernels: 30.9 us -> 31.4 us
    unnamed x7 -> x0, local copies, waits for them, and re-layouts: 3.91 us -> none
    broadcast_in_dim x2 -> x0, local copies, waits for them, and re-layouts: 2.59 us -> none  [the longest x1 1.29 us: body(): gain[None]]
    pallas_call x1 -> x2, Pallas kernels: 30.9 us -> 31.4 us  [the longest x1 30.2 us: body(): pl.pallas_call(functools.partial(kernel, dims), out_shape=(pltpu.VMEM(tok...]
where the time goes in v2:
time: 32.6 us; the launch traced here: 32 us
  Pallas kernels  31.4 us (96%)
  between operations  0.64 us (2%)
    pallas_call x1, Pallas kernels, body(): pl.pallas_call(functools.partial(kernel, dims), out_shape=(pltpu.VMEM(tok...  30.2 us
    pallas_call x1, Pallas kernels, body(): pl.pallas_call(write_out, out_shape=tuple((jax.ShapeDtypeStruct(o.shape,...  1.23 us

profile of v2, /device:TPU:1, one launch (start us, length us, event | category | flops | bytes accessed | tf_op | source)
XLA Modules:
  0.0 32.0 jit_solution(8893566304260749161)
XLA Ops:
  0.6 30.2 %shard_map.94 = (bf16[1,128,5120]{2,1,0:T(8,128)(2,1)S(1)}, bf16[1,128,1280]{2,1,0:T(8,128)(2,1)S(1)}, bf16[1,128,640]{2,1,0:T(8,128)(2,1)S(1)}) custom-call(bf16[1,128,640]{2,1,0:T(8,128)(2,1)} %mix_hbm.1, bf16[1,128,1280]{2,1,0:T(8,128)(2,1)} %resid_hbm.1, bf16[80,1280]{1,0:T(8,128)(2,1)} %w_hbm.1, f32[1280]{0:T(1024)} %gain_ref.1, f32[1280]{0:T(1024)} %bias_ref.1, ...), custom_call_target="tpu_custom_call" | custom-call | tf_op jit(solution)/shard_map/pallas_call | solution.py:325
  30.8 1.2 %shard_map.95 = (bf16[1,128,5120]{2,1,0:T(8,128)(2,1)}, bf16[1,128,1280]{2,1,0:T(8,128)(2,1)}, bf16[1,128,640]{2,1,0:T(8,128)(2,1)}) custom-call(bf16[1,128,5120]{2,1,0:T(8,128)(2,1)S(1)} %get-tuple-element.6.a_ref, bf16[1,128,1280]{2,1,0:T(8,128)(2,1)S(1)} %get-tuple-element.7.b_ref, bf16[1,128,640]{2,1,0:T(8,128)(2,1)S(1)} %get-tuple-element.8.c_ref), custom_call_target="tpu_custom_call" | custom-call | tf_op jit(solution)/shard_map/pallas_call | solution.py:352

commit v3 on v2

--- a/solution.py
+++ b/solution.py
@@ -25,14 +25,12 @@
     )
 
 
-def kernel(dims, mix_hbm, resid_hbm, w_hbm, gain_ref, bias_ref, target_ref, tg_hbm,
+def kernel(dims, mix_hbm, resid_hbm, w_hbm, gain_hbm, bias_hbm, target_hbm, tg_hbm,
            rows_s, rgrad_s, agrad_s,
-           mix, resid, tg, wbuf, bsend, brecv, fsend, frecv, xhat_s,
+           gain_ref, bias_ref, target_ref, mix, resid, tg, wbuf, bsend, brecv, fsend, frecv, xhat_s,
            load_sem, own_sem, zsend, ysend, psend, wrecv, precv, bs_sem, br_sem, fs_sem, fr_sem):
     S, D, A, B, cap, R, wcuts, fcuts = dims
     n_tok, wide = tg.shape
-    gain = gain_ref[...].reshape(1, -1)
-    bias = bias_ref[...].reshape(1, -1)
     patches, width = resid.shape
     M = target_ref.shape[1]
     merged = M // S
@@ -53,7 +51,11 @@
     tg_load = pltpu.make_async_copy(tg_hbm.at[0], tg, load_sem.at[0])
     mix_load = pltpu.make_async_copy(mix_hbm.at[0], mix, load_sem.at[1])
     resid_load = pltpu.make_async_copy(resid_hbm.at[0], resid, load_sem.at[2])
-    for c in loads + [tg_load, mix_load, resid_load]:
+    small = [
+        pltpu.make_async_copy(src, dst, load_sem.at[3 + i])
+        for i, (src, dst) in enumerate(((target_hbm, target_ref), (gain_hbm, gain_ref), (bias_hbm, bias_ref)))
+    ]
+    for c in loads + small[:1] + [tg_load, mix_load, resid_load] + small[1:]:
         c.start()
 
     barrier = pltpu.get_barrier_semaphore()
@@ -93,11 +95,11 @@
 
     def p_copy(shard, c):
         p = piece(h, shard, c)
-        return remote(p, p, psend.at[shard, c], precv.at[shard, c], {"seq": partner})
+        return remote(p, p, psend.at[0], precv.at[0], {"seq": partner})
 
     def arrived(shard, c):
         p = piece(h, shard, c)
-        remote(p, p, psend.at[shard, c], wrecv.at[shard, c], {"seq": partner}).wait_recv()
+        remote(p, p, psend.at[0], wrecv.at[shard, c], {"seq": partner}).wait_recv()
 
     def each_z(k, side, act):
         src = a + side * k
@@ -114,6 +116,7 @@
         for r in range(1, B):
             y_copy(a, r, c).start()
 
+    small[0].wait()
     t_row = target_ref[...].astype(F32)
     diag = iota((M, M), 0) == iota((M, M), 1)
     t_col = jnp.sum(jnp.where(diag, jnp.broadcast_to(t_row, (M, M)), 0.0), axis=1, keepdims=True)
@@ -205,19 +208,9 @@
         y_arrivals(k - 1)
     y_arrivals(A - 1)
 
-    def other_shards(act):
-        @pl.loop(0, D)
-        def _(shard):
-            @pl.when(shard != d)
-            def _():
-                for c in range(nc):
-                    act(shard, c)
-
-    def p_wait(shard, c):
-        p = piece(1 - h, shard, c)
-        remote(p, p, psend.at[shard, c], precv.at[shard, c], {"seq": partner}).wait_recv()
-
-    other_shards(p_wait)
+    def all_others(half_index):
+        p = wbuf.at[half_index, 0:D - 1]
+        return remote(p, p, psend.at[0], precv.at[0], {"seq": partner})
 
     def weight(i):
         if depth % 16 == 0:
@@ -226,10 +219,20 @@
 
     mix_load.wait()
     resid_load.wait()
+    for c in small[1:]:
+        c.wait()
+    gain = gain_ref[...].reshape(1, -1)
+    bias = bias_ref[...].reshape(1, -1)
+    for turn in range(2):
+        if turn == 1:
+            all_others(1 - h).wait_recv()
+        i = h if turn == 0 else 1 - h
+        columns = pl.ds(pl.multiple_of(i * half, 128), half)
+        xhat_s[:, columns] = resid[:, columns].astype(F32) + jnp.dot(
+            mix[...], weight(i), preferred_element_type=F32
+        )
+    hidden = xhat_s[...]
     w = [weight(i) for i in range(2)]
-    hidden = resid[...].astype(F32) + jnp.concatenate(
-        [jnp.dot(mix[...], w[i], preferred_element_type=F32) for i in range(2)], axis=1
-    )
     centered = hidden - jnp.mean(hidden, axis=-1, keepdims=True)
     rstd = lax.rsqrt(jnp.mean(centered * centered, axis=-1, keepdims=True) + EPS)
     xhat = centered * rstd
@@ -264,6 +267,17 @@
     )
     agrad_s[0] = agrad.astype(BF16)
 
+    for c in range(nc):
+        for side in (1, -1):
+            for k in range(A - 1):
+                each_z(k, side, lambda src, side=side, k=k, c=c: z_copy(src, side, k, c).wait_send())
+        for src in range(A):
+            for r in range(1, B):
+                y_copy(src, r, c).wait_send()
+    all_others(h).wait_send()
+    for r in range(1, S):
+        b_copy(r).wait_send()
+
     for c, (lo, hi) in enumerate(fcuts):
         for r in range(1, S):
             f_copy(c, S - r).wait_recv()
@@ -273,16 +287,7 @@
             part = (slice(None), slice(j * width + lo, j * width + hi))
             rows_s[(0,) + part] = placed[j * n_tok:(j + 1) * n_tok]
 
-    for c in range(nc):
-        for side in (1, -1):
-            for k in range(A - 1):
-                each_z(k, side, lambda src, side=side, k=k, c=c: z_copy(src, side, k, c).wait_send())
-        for src in range(A):
-            for r in range(1, B):
-                y_copy(src, r, c).wait_send()
-    other_shards(lambda shard, c: p_copy(shard, c).wait_send())
-    for r in range(1, S):
-        b_copy(r).wait_send()
+    for r in range(1, S):
         for c in range(len(fcuts)):
             f_copy(c, r).wait_send()
 
@@ -314,14 +319,14 @@
     A = D // B
     depth = out_weight.shape[0]
     wcuts = cuts(width // 2, 2)
-    fcuts = cuts(width, 5)
+    fcuts = cuts(width, 2)
     nc, nf = len(wcuts), len(fcuts)
     dims = (S, D, A, B, cap, R, wcuts, fcuts)
     hbm = pl.BlockSpec(memory_space=pltpu.HBM)
     vmem = pl.BlockSpec(memory_space=pltpu.VMEM)
     dma = pltpu.SemaphoreType.DMA
     result_bytes = 2 * (token_grad.size + resid.size + attn_mix.size)
-    grant = 60 * 1024 * 1024 - result_bytes - 320 * 1024
+    grant = 60 * 1024 * 1024 - result_bytes - 64 * 1024
     outs = pl.pallas_call(
         functools.partial(kernel, dims),
         out_shape=(
@@ -329,9 +334,12 @@
             pltpu.VMEM(resid.shape, BF16),
             pltpu.VMEM(attn_mix.shape, BF16),
         ),
-        in_specs=[hbm, hbm, hbm, vmem, vmem, vmem, hbm],
+        in_specs=[hbm] * 7,
         out_specs=(vmem, vmem, vmem),
         scratch_shapes=[
+            pltpu.VMEM(gain.shape, F32),
+            pltpu.VMEM(bias.shape, F32),
+            pltpu.VMEM(target.shape, jnp.int32),
             pltpu.VMEM((patches, columns), BF16),
             pltpu.VMEM((patches, width), BF16),
             pltpu.VMEM((n_tok, wide), BF16),
@@ -341,8 +349,8 @@
             pltpu.VMEM((S - 1, R // 8, 8, width), BF16),
             pltpu.VMEM((S, R // 8, 8, width), BF16),
             pltpu.VMEM((patches, width), F32),
-            dma((3,)), dma((2,)), dma((2, A - 1, nc)), dma((A, B - 1, nc)), dma((D, nc)),
-            dma((D, nc)), dma((D, nc)), dma((S - 1,)), dma((S - 1,)), dma((nf, S - 1)),
+            dma((6,)), dma((2,)), dma((2, A - 1, nc)), dma((A, B - 1, nc)), dma((1,)),
+            dma((D, nc)), dma((1,)), dma((S - 1,)), dma((S - 1,)), dma((nf, S - 1)),
             dma((nf, S - 1)),
         ],
         compiler_params=pltpu.CompilerParams(

time: 32.6 us -> 31.5 us (0.966); the launches traced: 32 us -> 31.4 us
  Pallas kernels: 31.4 us -> 30.7 us
    pallas_call x1, Pallas kernels: 30.2 us -> 29.5 us  [body(): pl.pallas_call(functools.partial(kernel, dims), out_shape=(pltpu.VMEM(tok...]
where the time goes in v3:
time: 31.5 us; the launch traced here: 31.4 us
  Pallas kernels  30.7 us (97%)
  between operations  0.64 us (2%)
    pallas_call x1, Pallas kernels, body(): pl.pallas_call(functools.partial(kernel, dims), out_shape=(pltpu.VMEM(tok...  29.5 us
    pallas_call x1, Pallas kernels, body(): pl.pallas_call(write_out, out_shape=tuple((jax.ShapeDtypeStruct(o.shape,...  1.23 us

profile of v3, /device:TPU:1, one launch (start us, length us, event | category | flops | bytes accessed | tf_op | source)
XLA Modules:
  0.0 31.4 jit_solution(18150717804020160669)
XLA Ops:
  0.6 29.5 %shard_map.94 = (bf16[1,128,5120]{2,1,0:T(8,128)(2,1)S(1)}, bf16[1,128,1280]{2,1,0:T(8,128)(2,1)S(1)}, bf16[1,128,640]{2,1,0:T(8,128)(2,1)S(1)}) custom-call(bf16[1,128,640]{2,1,0:T(8,128)(2,1)} %mix_hbm.1, bf16[1,128,1280]{2,1,0:T(8,128)(2,1)} %resid_hbm.1, bf16[80,1280]{1,0:T(8,128)(2,1)} %w_hbm.1, f32[1280]{0:T(1024)} %gain_hbm.1, f32[1280]{0:T(1024)} %bias_hbm.1, ...), custom_call_target="tpu_custom_call" | custom-call | tf_op jit(solution)/shard_map/pallas_call | solution.py:330
  30.1 1.2 %shard_map.95 = (bf16[1,128,5120]{2,1,0:T(8,128)(2,1)}, bf16[1,128,1280]{2,1,0:T(8,128)(2,1)}, bf16[1,128,640]{2,1,0:T(8,128)(2,1)}) custom-call(bf16[1,128,5120]{2,1,0:T(8,128)(2,1)S(1)} %get-tuple-element.6.a_ref, bf16[1,128,1280]{2,1,0:T(8,128)(2,1)S(1)} %get-tuple-element.7.b_ref, bf16[1,128,640]{2,1,0:T(8,128)(2,1)S(1)} %get-tuple-element.8.c_ref), custom_call_target="tpu_custom_call" | custom-call | tf_op jit(solution)/shard_map/pallas_call | solution.py:360

commit v4 on v3

--- a/solution.py
+++ b/solution.py
@@ -318,7 +318,7 @@
     B = 2 ** int(math.log2(D) // 2)
     A = D // B
     depth = out_weight.shape[0]
-    wcuts = cuts(width // 2, 2)
+    wcuts = cuts(width // 2, 5)
     fcuts = cuts(width, 2)
     nc, nf = len(wcuts), len(fcuts)
     dims = (S, D, A, B, cap, R, wcuts, fcuts)

time: 31.5 us -> 30.7 us (0.975)
  Pallas kernels: 30.7 us -> 29.9 us
    pallas_call x1, Pallas kernels: 29.5 us -> 28.7 us  [body(): pl.pallas_call(functools.partial(kernel, dims), out_shape=(pltpu.VMEM(tok...]
where the time goes in v4:
time: 30.7 us; the launch traced here: 30.5 us
  Pallas kernels  29.9 us (97%)
  between operations  0.64 us (2%)
    pallas_call x1, Pallas kernels, body(): pl.pallas_call(functools.partial(kernel, dims), out_shape=(pltpu.VMEM(tok...  28.7 us
    pallas_call x1, Pallas kernels, body(): pl.pallas_call(write_out, out_shape=tuple((jax.ShapeDtypeStruct(o.shape,...  1.23 us

profile of v4, /device:TPU:1, one launch (start us, length us, event | category | flops | bytes accessed | tf_op | source)
XLA Modules:
  0.0 30.5 jit_solution(14273354052557068025)
XLA Ops:
  0.6 28.7 %shard_map.94 = (bf16[1,128,5120]{2,1,0:T(8,128)(2,1)S(1)}, bf16[1,128,1280]{2,1,0:T(8,128)(2,1)S(1)}, bf16[1,128,640]{2,1,0:T(8,128)(2,1)S(1)}) custom-call(bf16[1,128,640]{2,1,0:T(8,128)(2,1)} %mix_hbm.1, bf16[1,128,1280]{2,1,0:T(8,128)(2,1)} %resid_hbm.1, bf16[80,1280]{1,0:T(8,128)(2,1)} %w_hbm.1, f32[1280]{0:T(1024)} %gain_hbm.1, f32[1280]{0:T(1024)} %bias_hbm.1, ...), custom_call_target="tpu_custom_call" | custom-call | tf_op jit(solution)/shard_map/pallas_call | solution.py:330
  29.3 1.2 %shard_map.95 = (bf16[1,128,5120]{2,1,0:T(8,128)(2,1)}, bf16[1,128,1280]{2,1,0:T(8,128)(2,1)}, bf16[1,128,640]{2,1,0:T(8,128)(2,1)}) custom-call(bf16[1,128,5120]{2,1,0:T(8,128)(2,1)S(1)} %get-tuple-element.6.a_ref, bf16[1,128,1280]{2,1,0:T(8,128)(2,1)S(1)} %get-tuple-element.7.b_ref, bf16[1,128,640]{2,1,0:T(8,128)(2,1)S(1)} %get-tuple-element.8.c_ref), custom_call_target="tpu_custom_call" | custom-call | tf_op jit(solution)/shard_map/pallas_call | solution.py:360
